TPU v7x, 512 devices: a whole 4x4x16 slice. The times are simulated.
512 devices in a mesh: cell: 32 (over x, y, core), blk: 16 (over z).
Axes of the slice: x: 4, y: 4, z: 16, core: 2. Of those that a mesh axis runs over, the one named last changes fastest.
Arguments:
- snapshots: float32 [512, 65536], P('blk', 'cell'), may hold values from -100 to 100
- plan: int32 [31, 32], replicated, may hold values from 0 to 31, as said below
Outputs:
- energy_field: float32 [512, 65536], P('blk', 'cell')
- mode_energy: float32 [512], P('blk')
Inputs may be any that keep to these rules, and one draw needn't show every extreme that they name: `plan`: each row pairs every index 0 .. 31 with exactly one other index (the partner's partner is the index itself, never the index), and over all rows every two indices are paired exactly once.
All inputs are finite; a program needn't handle non-finite values.
Results may differ from a plain program's by a relative error of at most 0.0055.
Values sent between devices are 32-bit elements; how exact they have to be, the bound alone decides.
A program may use at most 64 MiB of HBM per device.

v0:
```python
import jax
import jax.numpy as jnp
from jax import lax
from jax.sharding import PartitionSpec as P

ROUNDS = 7


def passed_along(value, axis, steps):
    count = lax.axis_size(axis)
    first, last = (max(0, -steps), min(count, count - steps))
    return lax.ppermute(value, axis, [(source, source + steps) for source in range(first, last)])


def inner_sweep(gram_whole, plan):
    pair_width = gram_whole.shape[0]
    positions = jnp.arange(pair_width, dtype=jnp.int32)

    def one_step(step_index, loop_state):
        gram_now, accumulated = loop_state
        partner = lax.dynamic_index_in_dim(plan, step_index, 0, keepdims=False)
        onehot = (partner[:, None] == positions[None, :]).astype(jnp.float32)
        symmetric = 0.5 * (gram_now + gram_now.T)
        own_diag = jnp.diagonal(symmetric)
        cross_term = jnp.sum(onehot * symmetric, axis=1)
        other_diag = jnp.sum(onehot * own_diag[None, :], axis=1)
        is_lower = positions < partner
        spread = jnp.where(is_lower, own_diag - other_diag, other_diag - own_diag)
        angles = 0.5 * jnp.arctan2(2.0 * cross_term, spread)
        cosine = jnp.cos(angles)
        sine_part = jnp.where(is_lower, jnp.sin(angles), -jnp.sin(angles))
        rotation_step = jnp.diag(cosine) + (onehot * sine_part[:, None]).T
        gram_now = jnp.dot(
            jnp.dot(rotation_step.T, gram_now, precision=lax.Precision.HIGHEST),
            rotation_step,
            precision=lax.Precision.HIGHEST,
        )
        accumulated = jnp.dot(accumulated, rotation_step, precision=lax.Precision.HIGHEST)
        return (gram_now, accumulated)

    initial = (gram_whole, jnp.eye(pair_width, dtype=jnp.float32))
    return lax.fori_loop(0, pair_width - 1, one_step, initial)[1]


def self_gram(block):
    return jnp.dot(block, block.T, precision=lax.Precision.HIGHEST)


def on_device(snapshots, plan):
    pair_width = snapshots.shape[0]
    half_width = pair_width // 2
    local_rows = snapshots.shape[1]
    block_devices = lax.axis_size("blk")
    position = lax.axis_index("blk")

    def round_step(round_index, loop_state):
        current, gram_local = loop_state
        gram_whole = lax.psum(gram_local, "cell")
        turning = inner_sweep(gram_whole, plan)
        rotated = jnp.dot(turning.T, current, precision=lax.Precision.HIGHEST)
        upper_part = rotated[:half_width]
        lower_part = rotated[half_width:]
        rightward = jnp.where(position == 0, lower_part, upper_part)
        from_left = passed_along(rightward, "blk", 1)
        from_right = passed_along(lower_part, "blk", -1)
        new_upper = jnp.where(position == 0, upper_part, from_left)
        new_lower = jnp.where(position == block_devices - 1, upper_part, from_right)
        current = jnp.concatenate([new_upper, new_lower], axis=0)
        gram_local = self_gram(current)
        return (current, gram_local)

    gram_first = self_gram(snapshots)
    current, gram_local = lax.fori_loop(0, ROUNDS, round_step, (snapshots, gram_first))
    squared = current * current
    energy_local = jnp.sum(squared, axis=1)
    total_rows = local_rows * lax.axis_size("cell")
    mode_energy = lax.psum(energy_local, "cell") / total_rows
    return (squared, mode_energy)


def solution(mesh):
    return jax.shard_map(
        on_device,
        mesh=mesh,
        in_specs=(P("blk", "cell"), P()),
        out_specs=(P("blk", "cell"), P("blk")),
        check_vma=False,
    )
```

profile of v0, /device:TPU:1, one launch (start us, length us, event | category | flops | bytes accessed | tf_op | source)
XLA Modules:
  0.0 1892.4 jit_solution(1336124570133756698)
XLA Ops:
  1.9 1820.3 %while.37 = (s32[]{:T(128)}, f32[32,2048]{1,0:T(8,128)S(1)}, f32[32,32]{1,0:T(8,128)S(1)}, pred[]{:T(512)}, s32[31,32]{1,0:T(8,128)}, /*index=5*/pred[]{:T(512)}, s32[]{:T(128)}, s32[]{:T(128)}, s32[]{:T(128)}) while((s32[]{:T(128)}, f32[32,2048]{1,0:T(8,128)S(1)}, f32[32,32]{1,0:T(8,128)S(1)}, pred[]{:T(512)}, s32[31,32]{1,0:T(8,128)}, ...), condition=%wide.region_6.7_spmd, body=%wide.region_0.6_spmd.sunk | while | flops 51701092 | bytes 3620785 | solution.py:73
  2.0 125.0 %psum.18 = f32[32,32]{1,0:T(8,128)S(1)} all-reduce(f32[32,32]{1,0:T(8,128)S(1)} %get-tuple-element.345), channel_id=1, replica_groups=mesh['cell'=32,'blk'=16] {'cell'}, use_global_device_ids=true, to_apply=%region_1.0 | all-reduce | flops 1024 | bytes 8192 | tf_op jit(solution)/shard_map/while/body/eval_jaxpr/psum | solution.py:58
  126.9 124.2 %while.38 = (s32[]{:T(128)}, f32[32,32]{1,0:T(8,128)S(1)}, f32[32,32]{0,1:T(8,128)S(1)}, s32[31,32]{1,0:T(8,128)}, s32[]{:T(128)}) while((s32[]{:T(128)}, f32[32,32]{1,0:T(8,128)S(1)}, f32[32,32]{0,1:T(8,128)S(1)}, s32[31,32]{1,0:T(8,128)}, s32[]{:T(128)}) %tuple.77), condition=%wide.region_5.5_spmd.clone.clone, body=%wide.region_2.4_spmd.clone.clone.sunk | while | flops 1202530 | bytes 61137 | solution.py:42
  260.6 125.0 %psum.18 = f32[32,32]{1,0:T(8,128)S(1)} all-reduce(f32[32,32]{1,0:T(8,128)S(1)} %get-tuple-element.345), channel_id=1, replica_groups=mesh['cell'=32,'blk'=16] {'cell'}, use_global_device_ids=true, to_apply=%region_1.0 | all-reduce | flops 1024 | bytes 8192 | tf_op jit(solution)/shard_map/while/body/eval_jaxpr/psum | solution.py:58
  385.6 124.2 %while.38 = (s32[]{:T(128)}, f32[32,32]{1,0:T(8,128)S(1)}, f32[32,32]{0,1:T(8,128)S(1)}, s32[31,32]{1,0:T(8,128)}, s32[]{:T(128)}) while((s32[]{:T(128)}, f32[32,32]{1,0:T(8,128)S(1)}, f32[32,32]{0,1:T(8,128)S(1)}, s32[31,32]{1,0:T(8,128)}, s32[]{:T(128)}) %tuple.77), condition=%wide.region_5.5_spmd.clone.clone, body=%wide.region_2.4_spmd.clone.clone.sunk | while | flops 1202530 | bytes 61137 | solution.py:42
  515.7 5.1 collective-permute-done.1
  521.2 124.9 %psum.18 = f32[32,32]{1,0:T(8,128)S(1)} all-reduce(f32[32,32]{1,0:T(8,128)S(1)} %get-tuple-element.345), channel_id=1, replica_groups=mesh['cell'=32,'blk'=16] {'cell'}, use_global_device_ids=true, to_apply=%region_1.0 | all-reduce | flops 1024 | bytes 8192 | tf_op jit(solution)/shard_map/while/body/eval_jaxpr/psum | solution.py:58
  646.1 124.2 %while.38 = (s32[]{:T(128)}, f32[32,32]{1,0:T(8,128)S(1)}, f32[32,32]{0,1:T(8,128)S(1)}, s32[31,32]{1,0:T(8,128)}, s32[]{:T(128)}) while((s32[]{:T(128)}, f32[32,32]{1,0:T(8,128)S(1)}, f32[32,32]{0,1:T(8,128)S(1)}, s32[31,32]{1,0:T(8,128)}, s32[]{:T(128)}) %tuple.77), condition=%wide.region_5.5_spmd.clone.clone, body=%wide.region_2.4_spmd.clone.clone.sunk | while | flops 1202530 | bytes 61137 | solution.py:42
  770.7 4.9 collective-permute-start
  777.5 4.1 collective-permute-done.1
  782.0 124.9 %psum.18 = f32[32,32]{1,0:T(8,128)S(1)} all-reduce(f32[32,32]{1,0:T(8,128)S(1)} %get-tuple-element.345), channel_id=1, replica_groups=mesh['cell'=32,'blk'=16] {'cell'}, use_global_device_ids=true, to_apply=%region_1.0 | all-reduce | flops 1024 | bytes 8192 | tf_op jit(solution)/shard_map/while/body/eval_jaxpr/psum | solution.py:58
  906.9 124.2 %while.38 = (s32[]{:T(128)}, f32[32,32]{1,0:T(8,128)S(1)}, f32[32,32]{0,1:T(8,128)S(1)}, s32[31,32]{1,0:T(8,128)}, s32[]{:T(128)}) while((s32[]{:T(128)}, f32[32,32]{1,0:T(8,128)S(1)}, f32[32,32]{0,1:T(8,128)S(1)}, s32[31,32]{1,0:T(8,128)}, s32[]{:T(128)}) %tuple.77), condition=%wide.region_5.5_spmd.clone.clone, body=%wide.region_2.4_spmd.clone.clone.sunk | while | flops 1202530 | bytes 61137 | solution.py:42
  1041.4 125.0 %psum.18 = f32[32,32]{1,0:T(8,128)S(1)} all-reduce(f32[32,32]{1,0:T(8,128)S(1)} %get-tuple-element.345), channel_id=1, replica_groups=mesh['cell'=32,'blk'=16] {'cell'}, use_global_device_ids=true, to_apply=%region_1.0 | all-reduce | flops 1024 | bytes 8192 | tf_op jit(solution)/shard_map/while/body/eval_jaxpr/psum | solution.py:58
  1166.4 124.2 %while.38 = (s32[]{:T(128)}, f32[32,32]{1,0:T(8,128)S(1)}, f32[32,32]{0,1:T(8,128)S(1)}, s32[31,32]{1,0:T(8,128)}, s32[]{:T(128)}) while((s32[]{:T(128)}, f32[32,32]{1,0:T(8,128)S(1)}, f32[32,32]{0,1:T(8,128)S(1)}, s32[31,32]{1,0:T(8,128)}, s32[]{:T(128)}) %tuple.77), condition=%wide.region_5.5_spmd.clone.clone, body=%wide.region_2.4_spmd.clone.clone.sunk | while | flops 1202530 | bytes 61137 | solution.py:42
  1291.0 4.5 collective-permute-start
  1297.4 4.1 collective-permute-done.1
  1301.9 124.9 %psum.18 = f32[32,32]{1,0:T(8,128)S(1)} all-reduce(f32[32,32]{1,0:T(8,128)S(1)} %get-tuple-element.345), channel_id=1, replica_groups=mesh['cell'=32,'blk'=16] {'cell'}, use_global_device_ids=true, to_apply=%region_1.0 | all-reduce | flops 1024 | bytes 8192 | tf_op jit(solution)/shard_map/while/body/eval_jaxpr/psum | solution.py:58
  1426.8 124.2 %while.38 = (s32[]{:T(128)}, f32[32,32]{1,0:T(8,128)S(1)}, f32[32,32]{0,1:T(8,128)S(1)}, s32[31,32]{1,0:T(8,128)}, s32[]{:T(128)}) while((s32[]{:T(128)}, f32[32,32]{1,0:T(8,128)S(1)}, f32[32,32]{0,1:T(8,128)S(1)}, s32[31,32]{1,0:T(8,128)}, s32[]{:T(128)}) %tuple.77), condition=%wide.region_5.5_spmd.clone.clone, body=%wide.region_2.4_spmd.clone.clone.sunk | while | flops 1202530 | bytes 61137 | solution.py:42
  1551.4 4.9 collective-permute-start
  1558.2 4.1 collective-permute-done.1
  1562.7 124.9 %psum.18 = f32[32,32]{1,0:T(8,128)S(1)} all-reduce(f32[32,32]{1,0:T(8,128)S(1)} %get-tuple-element.345), channel_id=1, replica_groups=mesh['cell'=32,'blk'=16] {'cell'}, use_global_device_ids=true, to_apply=%region_1.0 | all-reduce | flops 1024 | bytes 8192 | tf_op jit(solution)/shard_map/while/body/eval_jaxpr/psum | solution.py:58
  1687.6 124.2 %while.38 = (s32[]{:T(128)}, f32[32,32]{1,0:T(8,128)S(1)}, f32[32,32]{0,1:T(8,128)S(1)}, s32[31,32]{1,0:T(8,128)}, s32[]{:T(128)}) while((s32[]{:T(128)}, f32[32,32]{1,0:T(8,128)S(1)}, f32[32,32]{0,1:T(8,128)S(1)}, s32[31,32]{1,0:T(8,128)}, s32[]{:T(128)}) %tuple.77), condition=%wide.region_5.5_spmd.clone.clone, body=%wide.region_2.4_spmd.clone.clone.sunk | while | flops 1202530 | bytes 61137 | solution.py:42
  1817.7 4.1 collective-permute-done.1
  1823.1 68.8 %psum.16 = f32[32]{0:T(128)S(1)} all-reduce(f32[32]{0:T(128)S(1)} %get-tuple-element.224), channel_id=1, replica_groups=mesh['cell'=32,'blk'=16] {'cell'}, use_global_device_ids=true, to_apply=%region_8.9 | all-reduce | flops 32 | bytes 256 | tf_op jit(solution)/shard_map/psum | solution.py:77
  (2670 shorter events, 900.3 us)
Async XLA Ops:
  251.5 4.7 collective-permute-start
  254.3 5.9 collective-permute-start.1
  510.2 5.5 collective-permute-start
  513.8 7.0 collective-permute-start.1
  770.7 6.8 collective-permute-start
  775.5 6.0 collective-permute-start.1
  1031.4 5.6 collective-permute-start
  1035.1 5.9 collective-permute-start.1
  1291.0 6.4 collective-permute-start
  1295.5 6.0 collective-permute-start.1
  1551.4 6.8 collective-permute-start
  1556.2 6.0 collective-permute-start.1
  1812.2 5.6 collective-permute-start
  1815.8 6.0 collective-permute-start.1
where the time goes:
time: 1920 us; the launch traced here: 1890 us
  blocking collectives  943 us (49%)
  other arithmetic  370 us (19%)
  local copies, waits for them, and re-layouts  324 us (17%)
  matrix products  171 us (9%)
  starting transfers between devices  36.9 us (2%)
  waiting for transfers between devices  33.7 us (2%)
    psum x7, blocking collectives, round_step(): gram_whole = lax.psum(gram_local, 'cell')  875 us
    cos x217, other arithmetic, one_step(): cosine = jnp.cos(angles)  167 us
    select_n x217, other arithmetic, one_step(): sine_part = jnp.where(is_lower, jnp.sin(angles), -jnp.sin(angles))  159 us
    gather x217, local copies, waits for them, and re-layouts, one_step(): own_diag = jnp.diagonal(symmetric)  156 us
    eq x217, local copies, waits for them, and re-layouts, one_step(): onehot = (partner[:, None] == positions[None, :]).astype(jnp.float32)  151 us
    psum x1, blocking collectives, on_device(): mode_energy = lax.psum(energy_local, 'cell') / total_rows  68.8 us
    dot_general x217, matrix products, one_step(): jnp.dot(accumulated, rotation_step, precision=lax.Precision.HIGHEST)  60.8 us
    dot_general x217, matrix products, one_step(): jnp.dot(rotation_step.T, gram_now, precision=lax.Precision.HIGHEST)  60.1 us
  transfers between devices with their start and end apart: 14, of which 14 were waited for; matrix products, arithmetic and copies ran while one was open for 0% of the time, Pallas kernels for 0%

commit v1 on v0

--- a/solution.py
+++ b/solution.py
@@ -1,9 +1,18 @@
+import functools
 import jax
 import jax.numpy as jnp
 from jax import lax
 from jax.sharding import PartitionSpec as P
 
 ROUNDS = 7
+
+
+def compute_the_quotas(array_here, along_axis):
+    wide_out = lax.all_gather(array_here, along_axis).sum(axis=0)
+    return wide_out
+
+
+run_the_windows = functools.partial(compute_the_quotas, along_axis="cell")
 
 
 def passed_along(value, axis, steps):
@@ -74,7 +83,7 @@
     squared = current * current
     energy_local = jnp.sum(squared, axis=1)
     total_rows = local_rows * lax.axis_size("cell")
-    mode_energy = lax.psum(energy_local, "cell") / total_rows
+    mode_energy = run_the_windows(energy_local) / total_rows
     return (squared, mode_energy)
 
 

time: 1920 us -> 1920 us (level)
    unnamed x0 -> x1, blocking collectives: none -> 68.8 us
    psum x1 -> x0, blocking collectives: 68.8 us -> none  [on_device(): mode_energy = lax.psum(energy_local, 'cell') / total_rows]
where the time goes in v1:
time: 1920 us; the launch traced here: 1890 us
  blocking collectives  944 us (49%)
  other arithmetic  370 us (19%)
  local copies, waits for them, and re-layouts  325 us (17%)
  matrix products  170 us (9%)
  starting transfers between devices  36.9 us (2%)
  waiting for transfers between devices  33.7 us (2%)
    psum x7, blocking collectives, round_step(): gram_whole = lax.psum(gram_local, 'cell')  875 us
    cos x217, other arithmetic, one_step(): cosine = jnp.cos(angles)  167 us
    select_n x217, other arithmetic, one_step(): sine_part = jnp.where(is_lower, jnp.sin(angles), -jnp.sin(angles))  159 us
    gather x217, local copies, waits for them, and re-layouts, one_step(): own_diag = jnp.diagonal(symmetric)  155 us
    eq x217, local copies, waits for them, and re-layouts, one_step(): onehot = (partner[:, None] == positions[None, :]).astype(jnp.float32)  151 us
    unnamed x1, blocking collectives  68.8 us
    dot_general x217, matrix products, one_step(): jnp.dot(accumulated, rotation_step, precision=lax.Precision.HIGHEST)  60.1 us
    dot_general x217, matrix products, one_step(): jnp.dot(rotation_step.T, gram_now, precision=lax.Precision.HIGHEST)  60.1 us
  transfers between devices with their start and end apart: 14, of which 14 were waited for; matrix products, arithmetic and copies ran while one was open for 0% of the time, Pallas kernels for 0%

profile of v1, /device:TPU:1, one launch (start us, length us, event | category | flops | bytes accessed | tf_op | source)
XLA Modules:
  0.0 1893.9 jit_solution(2610574861932456558)
XLA Ops:
  1.9 1819.4 %while.37 = (s32[]{:T(128)}, f32[32,2048]{1,0:T(8,128)S(1)}, f32[32,32]{1,0:T(8,128)S(1)}, pred[]{:T(512)}, s32[31,32]{1,0:T(8,128)}, /*index=5*/pred[]{:T(512)}, s32[]{:T(128)}, s32[]{:T(128)}, s32[]{:T(128)}) while((s32[]{:T(128)}, f32[32,2048]{1,0:T(8,128)S(1)}, f32[32,32]{1,0:T(8,128)S(1)}, pred[]{:T(512)}, s32[31,32]{1,0:T(8,128)}, ...), condition=%wide.region_6.7_spmd, body=%wide.region_0.6_spmd.sunk | while | flops 51701092 | bytes 3620777 | solution.py:82
  2.0 125.0 %psum.10 = f32[32,32]{1,0:T(8,128)S(1)} all-reduce(f32[32,32]{1,0:T(8,128)S(1)} %get-tuple-element.345), channel_id=1, replica_groups=mesh['cell'=32,'blk'=16] {'cell'}, use_global_device_ids=true, to_apply=%region_1.0 | all-reduce | flops 1024 | bytes 8192 | tf_op jit(solution)/shard_map/while/body/eval_jaxpr/psum | solution.py:67
  126.9 124.0 %while.38 = (s32[]{:T(128)}, f32[32,32]{1,0:T(8,128)S(1)}, f32[32,32]{0,1:T(8,128)S(1)}, s32[31,32]{1,0:T(8,128)}, s32[]{:T(128)}) while((s32[]{:T(128)}, f32[32,32]{1,0:T(8,128)S(1)}, f32[32,32]{0,1:T(8,128)S(1)}, s32[31,32]{1,0:T(8,128)}, s32[]{:T(128)}) %tuple.77), condition=%wide.region_5.5_spmd.clone.clone, body=%wide.region_2.4_spmd.clone.clone.sunk | while | flops 1202530 | bytes 61129 | solution.py:51
  260.5 125.0 %psum.10 = f32[32,32]{1,0:T(8,128)S(1)} all-reduce(f32[32,32]{1,0:T(8,128)S(1)} %get-tuple-element.345), channel_id=1, replica_groups=mesh['cell'=32,'blk'=16] {'cell'}, use_global_device_ids=true, to_apply=%region_1.0 | all-reduce | flops 1024 | bytes 8192 | tf_op jit(solution)/shard_map/while/body/eval_jaxpr/psum | solution.py:67
  385.5 124.0 %while.38 = (s32[]{:T(128)}, f32[32,32]{1,0:T(8,128)S(1)}, f32[32,32]{0,1:T(8,128)S(1)}, s32[31,32]{1,0:T(8,128)}, s32[]{:T(128)}) while((s32[]{:T(128)}, f32[32,32]{1,0:T(8,128)S(1)}, f32[32,32]{0,1:T(8,128)S(1)}, s32[31,32]{1,0:T(8,128)}, s32[]{:T(128)}) %tuple.77), condition=%wide.region_5.5_spmd.clone.clone, body=%wide.region_2.4_spmd.clone.clone.sunk | while | flops 1202530 | bytes 61129 | solution.py:51
  515.4 5.1 collective-permute-done.1
  521.0 124.9 %psum.10 = f32[32,32]{1,0:T(8,128)S(1)} all-reduce(f32[32,32]{1,0:T(8,128)S(1)} %get-tuple-element.345), channel_id=1, replica_groups=mesh['cell'=32,'blk'=16] {'cell'}, use_global_device_ids=true, to_apply=%region_1.0 | all-reduce | flops 1024 | bytes 8192 | tf_op jit(solution)/shard_map/while/body/eval_jaxpr/psum | solution.py:67
  645.9 124.0 %while.38 = (s32[]{:T(128)}, f32[32,32]{1,0:T(8,128)S(1)}, f32[32,32]{0,1:T(8,128)S(1)}, s32[31,32]{1,0:T(8,128)}, s32[]{:T(128)}) while((s32[]{:T(128)}, f32[32,32]{1,0:T(8,128)S(1)}, f32[32,32]{0,1:T(8,128)S(1)}, s32[31,32]{1,0:T(8,128)}, s32[]{:T(128)}) %tuple.77), condition=%wide.region_5.5_spmd.clone.clone, body=%wide.region_2.4_spmd.clone.clone.sunk | while | flops 1202530 | bytes 61129 | solution.py:51
  770.3 4.9 collective-permute-start
  777.1 4.1 collective-permute-done.1
  781.6 124.9 %psum.10 = f32[32,32]{1,0:T(8,128)S(1)} all-reduce(f32[32,32]{1,0:T(8,128)S(1)} %get-tuple-element.345), channel_id=1, replica_groups=mesh['cell'=32,'blk'=16] {'cell'}, use_global_device_ids=true, to_apply=%region_1.0 | all-reduce | flops 1024 | bytes 8192 | tf_op jit(solution)/shard_map/while/body/eval_jaxpr/psum | solution.py:67
  906.5 124.0 %while.38 = (s32[]{:T(128)}, f32[32,32]{1,0:T(8,128)S(1)}, f32[32,32]{0,1:T(8,128)S(1)}, s32[31,32]{1,0:T(8,128)}, s32[]{:T(128)}) while((s32[]{:T(128)}, f32[32,32]{1,0:T(8,128)S(1)}, f32[32,32]{0,1:T(8,128)S(1)}, s32[31,32]{1,0:T(8,128)}, s32[]{:T(128)}) %tuple.77), condition=%wide.region_5.5_spmd.clone.clone, body=%wide.region_2.4_spmd.clone.clone.sunk | while | flops 1202530 | bytes 61129 | solution.py:51
  1041.0 125.0 %psum.10 = f32[32,32]{1,0:T(8,128)S(1)} all-reduce(f32[32,32]{1,0:T(8,128)S(1)} %get-tuple-element.345), channel_id=1, replica_groups=mesh['cell'=32,'blk'=16] {'cell'}, use_global_device_ids=true, to_apply=%region_1.0 | all-reduce | flops 1024 | bytes 8192 | tf_op jit(solution)/shard_map/while/body/eval_jaxpr/psum | solution.py:67
  1166.0 124.0 %while.38 = (s32[]{:T(128)}, f32[32,32]{1,0:T(8,128)S(1)}, f32[32,32]{0,1:T(8,128)S(1)}, s32[31,32]{1,0:T(8,128)}, s32[]{:T(128)}) while((s32[]{:T(128)}, f32[32,32]{1,0:T(8,128)S(1)}, f32[32,32]{0,1:T(8,128)S(1)}, s32[31,32]{1,0:T(8,128)}, s32[]{:T(128)}) %tuple.77), condition=%wide.region_5.5_spmd.clone.clone, body=%wide.region_2.4_spmd.clone.clone.sunk | while | flops 1202530 | bytes 61129 | solution.py:51
  1290.4 4.5 collective-permute-start
  1296.8 4.1 collective-permute-done.1
  1301.3 124.9 %psum.10 = f32[32,32]{1,0:T(8,128)S(1)} all-reduce(f32[32,32]{1,0:T(8,128)S(1)} %get-tuple-element.345), channel_id=1, replica_groups=mesh['cell'=32,'blk'=16] {'cell'}, use_global_device_ids=true, to_apply=%region_1.0 | all-reduce | flops 1024 | bytes 8192 | tf_op jit(solution)/shard_map/while/body/eval_jaxpr/psum | solution.py:67
  1426.3 124.0 %while.38 = (s32[]{:T(128)}, f32[32,32]{1,0:T(8,128)S(1)}, f32[32,32]{0,1:T(8,128)S(1)}, s32[31,32]{1,0:T(8,128)}, s32[]{:T(128)}) while((s32[]{:T(128)}, f32[32,32]{1,0:T(8,128)S(1)}, f32[32,32]{0,1:T(8,128)S(1)}, s32[31,32]{1,0:T(8,128)}, s32[]{:T(128)}) %tuple.77), condition=%wide.region_5.5_spmd.clone.clone, body=%wide.region_2.4_spmd.clone.clone.sunk | while | flops 1202530 | bytes 61129 | solution.py:51
  1550.7 4.9 collective-permute-start
  1557.5 4.1 collective-permute-done.1
  1562.0 124.9 %psum.10 = f32[32,32]{1,0:T(8,128)S(1)} all-reduce(f32[32,32]{1,0:T(8,128)S(1)} %get-tuple-element.345), channel_id=1, replica_groups=mesh['cell'=32,'blk'=16] {'cell'}, use_global_device_ids=true, to_apply=%region_1.0 | all-reduce | flops 1024 | bytes 8192 | tf_op jit(solution)/shard_map/while/body/eval_jaxpr/psum | solution.py:67
  1686.9 124.0 %while.38 = (s32[]{:T(128)}, f32[32,32]{1,0:T(8,128)S(1)}, f32[32,32]{0,1:T(8,128)S(1)}, s32[31,32]{1,0:T(8,128)}, s32[]{:T(128)}) while((s32[]{:T(128)}, f32[32,32]{1,0:T(8,128)S(1)}, f32[32,32]{0,1:T(8,128)S(1)}, s32[31,32]{1,0:T(8,128)}, s32[]{:T(128)}) %tuple.77), condition=%wide.region_5.5_spmd.clone.clone, body=%wide.region_2.4_spmd.clone.clone.sunk | while | flops 1202530 | bytes 61129 | solution.py:51
  1816.9 4.1 collective-permute-done.1
  1824.4 68.8 %all-reduce = f32[1024]{0:T(1024)S(1)} all-reduce(f32[1024]{0:T(1024)S(1)} %dynamic-update-slice), channel_id=2, replica_groups=mesh['cell'=32,'blk'=16] {'cell'}, use_global_device_ids=true, to_apply=%add | all-reduce | flops 1024 | bytes 8192
  (2675 shorter events, 900.2 us)
Async XLA Ops:
  251.3 4.7 collective-permute-start
  254.2 5.9 collective-permute-start.1
  510.0 5.5 collective-permute-start
  513.5 7.0 collective-permute-start.1
  770.3 6.8 collective-permute-start
  775.2 6.0 collective-permute-start.1
  1031.0 5.6 collective-permute-start
  1034.6 5.9 collective-permute-start.1
  1290.4 6.4 collective-permute-start
  1294.9 6.0 collective-permute-start.1
  1550.7 6.8 collective-permute-start
  1555.5 6.0 collective-permute-start.1
  1811.3 5.6 collective-permute-start
  1815.0 6.0 collective-permute-start.1
